TPU v7x, 32 devices: a whole 2x2x4 slice. The times are simulated.
32 devices in a mesh: dom: 8 (over z, core), rep: 4 (over y, x).
Axes of the slice: x: 2, y: 2, z: 4, core: 2. Of those that a mesh axis runs over, the one named last changes fastest.
Arguments:
- node_features: bfloat16 [16384, 256], P(('dom', 'rep')), may hold values from -6 to 6
- weight: bfloat16 [256, 256], replicated, may hold values from -0.375 to 0.375
- cotangent: bfloat16 [16384, 256], P(('dom', 'rep')), may hold values from -6 to 6
- tile_row: int32 [8, 4, 512], P('dom', 'rep'), may hold values from 0 to 15
- tile_col: int32 [8, 4, 512], P('dom', 'rep'), may hold values from 0 to 31
- tile_values: bfloat16 [8, 4, 512, 128, 128], P('dom', 'rep'), may hold values from -0.0625 to 0.0625
- tile_count: int32 [8, 4], P('dom', 'rep'), may hold values from 128 to 512, as said below
Outputs:
- output: bfloat16 [16384, 256], P(('dom', 'rep'))
- grad_features: bfloat16 [16384, 256], P(('dom', 'rep'))
- grad_weight: float32 [256, 256], replicated
Inputs may be any that keep to these rules, and one draw needn't show every extreme that they name: Live slots are the first tile_count slots of each device's list; some device has all 512 slots live.
All inputs are finite; a program needn't handle non-finite values.
Results may differ from a plain program's by a relative error of at most 0.0061.
Values may be sent and summed in bfloat16 or wider, within the bound.
A program may use at most 192 MiB of HBM per device.

v0:
```python
import jax
import jax.numpy as jnp
from jax import lax
from jax.sharding import PartitionSpec as P


def silu_slope(summed):
    sig = jax.nn.sigmoid(summed)
    return sig * (1.0 + summed * (1.0 - sig))


def tile_products(values, pick_index, place_index, active, source, out_blocks, flipped):
    slots = values.shape[0]
    feature_width = source.shape[2]
    per_turn = min(slots, 128)
    pattern = "tba,tbf->taf" if flipped else "tab,tbf->taf"

    def accumulate(turn_index, summed):
        first_slot = turn_index * per_turn
        block_values = lax.dynamic_slice_in_dim(values, first_slot, per_turn, 0)
        picks = lax.dynamic_slice_in_dim(pick_index, first_slot, per_turn, 0)
        picked = jnp.take(source, picks, axis=0)
        products = jnp.einsum(pattern, block_values, picked, preferred_element_type=jnp.float32)
        places = lax.dynamic_slice_in_dim(place_index, first_slot, per_turn, 0)
        enabled = lax.dynamic_slice_in_dim(active, first_slot, per_turn, 0)
        products = products * enabled.astype(jnp.float32)[:, None, None]
        return summed.at[places].add(products)

    initial = jnp.zeros((out_blocks, 128, feature_width), jnp.float32)
    summed = lax.fori_loop(0, slots // per_turn, accumulate, initial)
    return summed.reshape(out_blocks * 128, feature_width)


def body(node_features, weight, cotangent, tile_row, tile_col, tile_values, tile_count):
    rows_here = node_features.shape[0]
    feature_width = weight.shape[0]
    dom_size = lax.axis_size("dom")
    rep_size = lax.axis_size("rep")
    slots = tile_row.shape[2]
    row_index = tile_row.reshape(slots)
    col_index = tile_col.reshape(slots)
    values = tile_values.reshape(slots, 128, 128)
    active = lax.broadcasted_iota(jnp.int32, (slots,), 0) < tile_count.reshape(())
    raw_rows = lax.all_gather(node_features, "dom", axis=0, tiled=True)
    gathered = jnp.dot(raw_rows, weight, preferred_element_type=jnp.float32).astype(jnp.bfloat16)
    source = gathered.reshape(-1, 128, feature_width)
    part_blocks = rep_size * rows_here // 128
    partial_value = tile_products(values, col_index, row_index, active, source, part_blocks, False)
    summed = lax.psum_scatter(partial_value, "rep", scatter_dimension=0, tiled=True)
    output = jax.nn.silu(summed).astype(jnp.bfloat16)
    grad_own = (cotangent.astype(jnp.float32) * silu_slope(summed)).astype(jnp.bfloat16)
    grad_block = lax.all_gather(grad_own, "rep", axis=0, tiled=True)
    back_blocks = dom_size * rows_here // 128
    back_partial = tile_products(
        values,
        row_index,
        col_index,
        active,
        grad_block.reshape(-1, 128, feature_width),
        back_blocks,
        True,
    )
    grad_projected = lax.psum_scatter(back_partial, "dom", scatter_dimension=0, tiled=True).astype(
        jnp.bfloat16
    )
    grad_features = jnp.dot(grad_projected, weight.T, preferred_element_type=jnp.float32).astype(
        jnp.bfloat16
    )
    local_weight = jnp.dot(node_features.T, grad_projected, preferred_element_type=jnp.float32)
    grad_weight = lax.psum(local_weight, ("dom", "rep"))
    return (output, grad_features, grad_weight)


def solution(mesh):
    placed = (
        P(("dom", "rep"), None),
        P(),
        P(("dom", "rep"), None),
        P("dom", "rep", None),
        P("dom", "rep", None),
        P("dom", "rep", None, None, None),
        P("dom", "rep"),
    )
    return jax.shard_map(
        body,
        mesh=mesh,
        in_specs=placed,
        out_specs=(P(("dom", "rep"), None), P(("dom", "rep"), None), P()),
        check_vma=False,
    )
```

profile of v0, /device:TPU:0, one launch (start us, length us, event | category | flops | bytes accessed | tf_op | source)
XLA Modules:
  0.0 719.0 jit_solution(10474179831010498034)
XLA Ops:
  7.2 0.7 all-gather.3.cloned.1.call-update
  8.6 32.9 %all-gather.3.cloned.1.call-done = bf16[4096,256]{1,0:T(8,128)(2,1)} async-done(((bf16[512,256]{1,0:T(8,128)(2,1)}), bf16[4096,256]{1,0:T(8,128)(2,1)}) %all-gather.3.cloned.1.call-update) | async-done | bytes 2097168 | tf_op jit(solution)/shard_map/all_gather | solution.py:44
  41.5 3.7 convolution_convert_fusion
  45.2 0.2 broadcast_in_dim.74
  45.4 181.9 %while.26 = (s32[]{:T(128)}, f32[16,128,256]{2,1,0:T(8,128)S(1)}, s32[512]{0:T(512)S(1)}, bf16[512,128,128]{2,1,0:T(8,128)(2,1)}, s32[512]{0:T(512)S(1)}, /*inde...) while((s32[]{:T(128)}, f32[16,128,256]{2,1,0:T(8,128)S(1)}, ...), condition=%wide.region_2.3_spmd, body=%wide.region_0.2_spmd.sunk | while | flops 1086327040 | bytes 96478248 | solution.py:30
  45.4 0.1 compare_and_fusion.4
  45.5 8.2 %gather_fusion = bf16[128,128,256]{2,1,0:T(8,128)(2,1)} fusion(bf16[32,128,256]{2,1,0:T(8,128)(2,1)} %get-tuple-element.424, s32[1024]{0:T(1024)S(1)} %pad_clamp_fusion.4), kind=kCustom, calls=%fused_computation.clone.1 | custom fusion | bytes 16777728 | tf_op jit(solution)/shard_map/while/body/eval_jaxpr/jit(_take)/gather | solution.py:22
  53.7 12.8 %convolution_multiply_fusion.4 = f32[128,128,256]{2,1,0:T(8,128)} fusion(f32[128]{0:T(128)S(1)} %get-tuple-element.384, bf16[128,128,256]{2,1,0:T(8,128)(2,1)} %gather_fusion, pred[128]{0:T(512)(128)(4,1)S(1)} %get-tuple-element.386, bf16[512,128,128]{2,1,0:T(8,128)(2,1)} %get-tuple-element.422, s32[]{:T(128)S(6)} %select_n.85), kind=kOutput, calls=%fused_computation.4.clone.1 | convolution fusion | flops 1082130432 | bytes 29360772 | tf_op jit(solution)/shard_map/while/body/eval_jaxpr/tab,tbf->taf/dot_general | solution.py:23
  66.6 24.3 %scatter_fusion = f32[16,128,256]{2,1,0:T(8,128)S(1)} fusion(f32[16,128,256]{2,1,0:T(8,128)S(1)} %get-tuple-element.409, s32[128]{0:T(128)S(1)} %compare_select_fusion.8, f32[128,128,256]{2,1,0:T(8,128)} %convolution_multiply_fusion.4), kind=kCustom, calls=%fused_computation.2.clone.1 | custom fusion | flops 4194304 | bytes 50332160 | tf_op jit(solution)/shard_map/while/body/eval_jaxpr/scatter-add | solution.py:27
  90.9 0.1 compare_and_fusion.4
  91.0 8.2 %gather_fusion = bf16[128,128,256]{2,1,0:T(8,128)(2,1)} fusion(bf16[32,128,256]{2,1,0:T(8,128)(2,1)} %get-tuple-element.424, s32[1024]{0:T(1024)S(1)} %pad_clamp_fusion.4), kind=kCustom, calls=%fused_computation.clone.1 | custom fusion | bytes 16777728 | tf_op jit(solution)/shard_map/while/body/eval_jaxpr/jit(_take)/gather | solution.py:22
  99.2 12.8 %convolution_multiply_fusion.4 = f32[128,128,256]{2,1,0:T(8,128)} fusion(f32[128]{0:T(128)S(1)} %get-tuple-element.384, bf16[128,128,256]{2,1,0:T(8,128)(2,1)} %gather_fusion, pred[128]{0:T(512)(128)(4,1)S(1)} %get-tuple-element.386, bf16[512,128,128]{2,1,0:T(8,128)(2,1)} %get-tuple-element.422, s32[]{:T(128)S(6)} %select_n.85), kind=kOutput, calls=%fused_computation.4.clone.1 | convolution fusion | flops 1082130432 | bytes 29360772 | tf_op jit(solution)/shard_map/while/body/eval_jaxpr/tab,tbf->taf/dot_general | solution.py:23
  112.1 24.3 %scatter_fusion = f32[16,128,256]{2,1,0:T(8,128)S(1)} fusion(f32[16,128,256]{2,1,0:T(8,128)S(1)} %get-tuple-element.409, s32[128]{0:T(128)S(1)} %compare_select_fusion.8, f32[128,128,256]{2,1,0:T(8,128)} %convolution_multiply_fusion.4), kind=kCustom, calls=%fused_computation.2.clone.1 | custom fusion | flops 4194304 | bytes 50332160 | tf_op jit(solution)/shard_map/while/body/eval_jaxpr/scatter-add | solution.py:27
  136.4 0.1 compare_and_fusion.4
  136.5 8.2 %gather_fusion = bf16[128,128,256]{2,1,0:T(8,128)(2,1)} fusion(bf16[32,128,256]{2,1,0:T(8,128)(2,1)} %get-tuple-element.424, s32[1024]{0:T(1024)S(1)} %pad_clamp_fusion.4), kind=kCustom, calls=%fused_computation.clone.1 | custom fusion | bytes 16777728 | tf_op jit(solution)/shard_map/while/body/eval_jaxpr/jit(_take)/gather | solution.py:22
  144.7 12.8 %convolution_multiply_fusion.4 = f32[128,128,256]{2,1,0:T(8,128)} fusion(f32[128]{0:T(128)S(1)} %get-tuple-element.384, bf16[128,128,256]{2,1,0:T(8,128)(2,1)} %gather_fusion, pred[128]{0:T(512)(128)(4,1)S(1)} %get-tuple-element.386, bf16[512,128,128]{2,1,0:T(8,128)(2,1)} %get-tuple-element.422, s32[]{:T(128)S(6)} %select_n.85), kind=kOutput, calls=%fused_computation.4.clone.1 | convolution fusion | flops 1082130432 | bytes 29360772 | tf_op jit(solution)/shard_map/while/body/eval_jaxpr/tab,tbf->taf/dot_general | solution.py:23
  157.6 24.3 %scatter_fusion = f32[16,128,256]{2,1,0:T(8,128)S(1)} fusion(f32[16,128,256]{2,1,0:T(8,128)S(1)} %get-tuple-element.409, s32[128]{0:T(128)S(1)} %compare_select_fusion.8, f32[128,128,256]{2,1,0:T(8,128)} %convolution_multiply_fusion.4), kind=kCustom, calls=%fused_computation.2.clone.1 | custom fusion | flops 4194304 | bytes 50332160 | tf_op jit(solution)/shard_map/while/body/eval_jaxpr/scatter-add | solution.py:27
  181.9 0.1 compare_and_fusion.4
  182.0 8.2 %gather_fusion = bf16[128,128,256]{2,1,0:T(8,128)(2,1)} fusion(bf16[32,128,256]{2,1,0:T(8,128)(2,1)} %get-tuple-element.424, s32[1024]{0:T(1024)S(1)} %pad_clamp_fusion.4), kind=kCustom, calls=%fused_computation.clone.1 | custom fusion | bytes 16777728 | tf_op jit(solution)/shard_map/while/body/eval_jaxpr/jit(_take)/gather | solution.py:22
  190.2 12.8 %convolution_multiply_fusion.4 = f32[128,128,256]{2,1,0:T(8,128)} fusion(f32[128]{0:T(128)S(1)} %get-tuple-element.384, bf16[128,128,256]{2,1,0:T(8,128)(2,1)} %gather_fusion, pred[128]{0:T(512)(128)(4,1)S(1)} %get-tuple-element.386, bf16[512,128,128]{2,1,0:T(8,128)(2,1)} %get-tuple-element.422, s32[]{:T(128)S(6)} %select_n.85), kind=kOutput, calls=%fused_computation.4.clone.1 | convolution fusion | flops 1082130432 | bytes 29360772 | tf_op jit(solution)/shard_map/while/body/eval_jaxpr/tab,tbf->taf/dot_general | solution.py:23
  203.1 24.3 %scatter_fusion = f32[16,128,256]{2,1,0:T(8,128)S(1)} fusion(f32[16,128,256]{2,1,0:T(8,128)S(1)} %get-tuple-element.409, s32[128]{0:T(128)S(1)} %compare_select_fusion.8, f32[128,128,256]{2,1,0:T(8,128)} %convolution_multiply_fusion.4), kind=kCustom, calls=%fused_computation.2.clone.1 | custom fusion | flops 4194304 | bytes 50332160 | tf_op jit(solution)/shard_map/while/body/eval_jaxpr/scatter-add | solution.py:27
  227.4 1.3 copy-done.1
  228.8 34.6 %reduce-scatter.3.cloned.1.call-done = f32[512,256]{1,0:T(8,128)} async-done(((f32[2048,256]{1,0:T(8,128)}), f32[512,256]{1,0:T(8,128)}) %reduce-scatter.3.cloned.1.call-update) | async-done | bytes 524304 | tf_op jit(solution)/shard_map/reduce_scatter | solution.py:49
  263.4 2.1 multiply_convert_fusion
  265.5 0.2 reduce-scatter.5.cloned.1.call-start
  265.7 22.4 %copy.10 = bf16[1,1,512,128,128]{3,4,2,1,0:T(8,128)(2,1)} copy(bf16[1,1,512,128,128]{4,3,2,1,0:T(8,128)(2,1)} %bitcast.21) | data formatting | bytes 33554432 | tf_op args[5]
  288.1 4.3 all-gather.5.cloned.1.call-done
  292.4 2.4 broadcast_in_dim.75
  294.8 234.0 %while.27 = (s32[]{:T(128)}, f32[32,128,256]{2,1,0:T(8,128)}, s32[512]{0:T(512)S(1)}, bf16[512,128,128]{1,2,0:T(8,128)(2,1)}, s32[512]{0:T(512)S(1)}, /*index=5*...) while((s32[]{:T(128)}, f32[32,128,256]{2,1,0:T(8,128)}, ...), condition=%wide.region_6.7_spmd, body=%wide.region_4.6_spmd.sunk | while | flops 1086327040 | bytes 96478248 | solution.py:30
  294.8 0.1 compare_and_fusion.5
  294.9 7.8 %gather_fusion.1 = bf16[128,128,256]{2,1,0:T(8,128)(2,1)} fusion(bf16[16,128,256]{2,1,0:T(8,128)(2,1)} %get-tuple-element.457, s32[1024]{0:T(1024)S(1)} %pad_clamp_fusion.5), kind=kCustom, calls=%fused_computation.1.clone.1 | custom fusion | bytes 16777728 | tf_op jit(solution)/shard_map/while/body/eval_jaxpr/jit(_take)/gather | solution.py:22
  302.7 12.8 %convolution_multiply_fusion.5 = f32[128,128,256]{2,1,0:T(8,128)} fusion(f32[128]{0:T(128)S(1)} %get-tuple-element.394, bf16[128,128,256]{2,1,0:T(8,128)(2,1)} %gather_fusion.1, pred[128]{0:T(512)(128)(4,1)S(1)} %get-tuple-element.396, bf16[512,128,128]{1,2,0:T(8,128)(2,1)} %get-tuple-element.455, s32[]{:T(128)S(6)} %select_n.88), kind=kOutput, calls=%fused_computation.16.clone.1 | convolution fusion | flops 1082130432 | bytes 29360772 | tf_op jit(solution)/shard_map/while/body/eval_jaxpr/tba,tbf->taf/dot_general | solution.py:23
  315.5 37.9 %scatter_fusion.1 = f32[32,128,256]{2,1,0:T(8,128)} fusion(f32[32,128,256]{2,1,0:T(8,128)} %get-tuple-element.442, s32[128]{0:T(128)S(1)} %compare_select_fusion.9, f32[128,128,256]{2,1,0:T(8,128)} %convolution_multiply_fusion.5), kind=kCustom, calls=%fused_computation.3.clone.1 | custom fusion | flops 4194304 | bytes 50332160 | tf_op jit(solution)/shard_map/while/body/eval_jaxpr/scatter-add | solution.py:27
  353.5 7.8 %gather_fusion.1 = bf16[128,128,256]{2,1,0:T(8,128)(2,1)} fusion(bf16[16,128,256]{2,1,0:T(8,128)(2,1)} %get-tuple-element.457, s32[1024]{0:T(1024)S(1)} %pad_clamp_fusion.5), kind=kCustom, calls=%fused_computation.1.clone.1 | custom fusion | bytes 16777728 | tf_op jit(solution)/shard_map/while/body/eval_jaxpr/jit(_take)/gather | solution.py:22
  361.2 12.8 %convolution_multiply_fusion.5 = f32[128,128,256]{2,1,0:T(8,128)} fusion(f32[128]{0:T(128)S(1)} %get-tuple-element.394, bf16[128,128,256]{2,1,0:T(8,128)(2,1)} %gather_fusion.1, pred[128]{0:T(512)(128)(4,1)S(1)} %get-tuple-element.396, bf16[512,128,128]{1,2,0:T(8,128)(2,1)} %get-tuple-element.455, s32[]{:T(128)S(6)} %select_n.88), kind=kOutput, calls=%fused_computation.16.clone.1 | convolution fusion | flops 1082130432 | bytes 29360772 | tf_op jit(solution)/shard_map/while/body/eval_jaxpr/tba,tbf->taf/dot_general | solution.py:23
  374.1 37.7 %scatter_fusion.1 = f32[32,128,256]{2,1,0:T(8,128)} fusion(f32[32,128,256]{2,1,0:T(8,128)} %get-tuple-element.442, s32[128]{0:T(128)S(1)} %compare_select_fusion.9, f32[128,128,256]{2,1,0:T(8,128)} %convolution_multiply_fusion.5), kind=kCustom, calls=%fused_computation.3.clone.1 | custom fusion | flops 4194304 | bytes 50332160 | tf_op jit(solution)/shard_map/while/body/eval_jaxpr/scatter-add | solution.py:27
  411.9 7.8 %gather_fusion.1 = bf16[128,128,256]{2,1,0:T(8,128)(2,1)} fusion(bf16[16,128,256]{2,1,0:T(8,128)(2,1)} %get-tuple-element.457, s32[1024]{0:T(1024)S(1)} %pad_clamp_fusion.5), kind=kCustom, calls=%fused_computation.1.clone.1 | custom fusion | bytes 16777728 | tf_op jit(solution)/shard_map/while/body/eval_jaxpr/jit(_take)/gather | solution.py:22
  419.7 12.8 %convolution_multiply_fusion.5 = f32[128,128,256]{2,1,0:T(8,128)} fusion(f32[128]{0:T(128)S(1)} %get-tuple-element.394, bf16[128,128,256]{2,1,0:T(8,128)(2,1)} %gather_fusion.1, pred[128]{0:T(512)(128)(4,1)S(1)} %get-tuple-element.396, bf16[512,128,128]{1,2,0:T(8,128)(2,1)} %get-tuple-element.455, s32[]{:T(128)S(6)} %select_n.88), kind=kOutput, calls=%fused_computation.16.clone.1 | convolution fusion | flops 1082130432 | bytes 29360772 | tf_op jit(solution)/shard_map/while/body/eval_jaxpr/tba,tbf->taf/dot_general | solution.py:23
  432.6 37.6 %scatter_fusion.1 = f32[32,128,256]{2,1,0:T(8,128)} fusion(f32[32,128,256]{2,1,0:T(8,128)} %get-tuple-element.442, s32[128]{0:T(128)S(1)} %compare_select_fusion.9, f32[128,128,256]{2,1,0:T(8,128)} %convolution_multiply_fusion.5), kind=kCustom, calls=%fused_computation.3.clone.1 | custom fusion | flops 4194304 | bytes 50332160 | tf_op jit(solution)/shard_map/while/body/eval_jaxpr/scatter-add | solution.py:27
  470.2 0.1 compare_and_fusion.5
  470.3 7.8 %gather_fusion.1 = bf16[128,128,256]{2,1,0:T(8,128)(2,1)} fusion(bf16[16,128,256]{2,1,0:T(8,128)(2,1)} %get-tuple-element.457, s32[1024]{0:T(1024)S(1)} %pad_clamp_fusion.5), kind=kCustom, calls=%fused_computation.1.clone.1 | custom fusion | bytes 16777728 | tf_op jit(solution)/shard_map/while/body/eval_jaxpr/jit(_take)/gather | solution.py:22
  478.0 12.8 %convolution_multiply_fusion.5 = f32[128,128,256]{2,1,0:T(8,128)} fusion(f32[128]{0:T(128)S(1)} %get-tuple-element.394, bf16[128,128,256]{2,1,0:T(8,128)(2,1)} %gather_fusion.1, pred[128]{0:T(512)(128)(4,1)S(1)} %get-tuple-element.396, bf16[512,128,128]{1,2,0:T(8,128)(2,1)} %get-tuple-element.455, s32[]{:T(128)S(6)} %select_n.88), kind=kOutput, calls=%fused_computation.16.clone.1 | convolution fusion | flops 1082130432 | bytes 29360772 | tf_op jit(solution)/shard_map/while/body/eval_jaxpr/tba,tbf->taf/dot_general | solution.py:23
  490.9 37.9 %scatter_fusion.1 = f32[32,128,256]{2,1,0:T(8,128)} fusion(f32[32,128,256]{2,1,0:T(8,128)} %get-tuple-element.442, s32[128]{0:T(128)S(1)} %compare_select_fusion.9, f32[128,128,256]{2,1,0:T(8,128)} %convolution_multiply_fusion.5), kind=kCustom, calls=%fused_computation.3.clone.1 | custom fusion | flops 4194304 | bytes 50332160 | tf_op jit(solution)/shard_map/while/body/eval_jaxpr/scatter-add | solution.py:27
  528.8 50.8 %reduce-scatter.5.cloned.1.call-done = f32[512,256]{1,0:T(8,128)} async-done(((f32[4096,256]{1,0:T(8,128)}), f32[512,256]{1,0:T(8,128)}) %reduce-scatter.5.cloned.1.call-update) | async-done | bytes 524304 | tf_op jit(solution)/shard_map/reduce_scatter | solution.py:63
  579.6 2.0 convolution_bitcast_fusion
  581.6 2.0 convolution_convert_fusion.1
  583.7 127.0 %all-reduce.2.cloned.1.call-done = f32[256,256]{0,1:T(8,128)} async-done(((f32[256,256]{0,1:T(8,128)}), f32[256,256]{0,1:T(8,128)}) %all-reduce.2.cloned.1.call-update) | async-done | bytes 262160 | tf_op jit(solution)/shard_map/psum | solution.py:70
  710.6 1.8 copy.12
  (38 shorter events, 1.1 us)
Async XLA Ops:
  7.2 34.4 %copy-start = (bf16[256,256]{1,0:T(8,128)(2,1)S(1)}, bf16[256,256]{1,0:T(8,128)(2,1)}, u32[]{:S(2)}) copy-start(bf16[256,256]{1,0:T(8,128)(2,1)} %param.12) | copy-start | bytes 393220
  7.2 38.2 %copy-start.4 = (s32[1,1,512]{2,1,0:T(1,128)S(1)}, s32[1,1,512]{2,1,0:T(1,128)}, u32[]{:S(2)}) copy-start(s32[1,1,512]{2,1,0:T(1,128)} %param.14) | copy-start | bytes 6148
  7.2 38.2 %copy-start.5 = (s32[1,1,512]{2,1,0:T(1,128)S(1)}, s32[1,1,512]{2,1,0:T(1,128)}, u32[]{:S(2)}) copy-start(s32[1,1,512]{2,1,0:T(1,128)} %param.15) | copy-start | bytes 6148
  7.2 34.3 %all-gather.3.cloned.1.call-start = ((), (), s32[]{:S(2)}) async-start(), calls=%async_computation.2 | async-start | bytes 2359296 | tf_op jit(solution)/shard_map/all_gather | solution.py:44
  7.9 255.5 %reduce-scatter.3.cloned.1.call-start = ((), (), s32[]{:S(2)}) async-start(), calls=%async_computation.3 | async-start | bytes 2621440 | tf_op jit(solution)/shard_map/reduce_scatter | solution.py:49
  45.4 218.0 %copy-start.3 = (bf16[512,256]{1,0:T(8,128)(2,1)S(1)}, bf16[512,256]{1,0:T(8,128)(2,1)}, u32[]{:S(2)}) copy-start(bf16[512,256]{1,0:T(8,128)(2,1)} %param.13) | copy-start | bytes 786436
  227.4 1.3 copy-start.1
  228.7 63.6 %all-gather.5.cloned.1.call-start = ((), (), s32[]{:S(2)}) async-start(), calls=%async_computation.4 | async-start | bytes 1310720 | tf_op jit(solution)/shard_map/all_gather | solution.py:52
  265.5 314.1 %reduce-scatter.5.cloned.1.call-start = ((), (), s32[]{:S(2)}) async-start(), calls=%async_computation.5 | async-start | bytes 4718592 | tf_op jit(solution)/shard_map/reduce_scatter | solution.py:63
  294.8 284.8 %copy-start.2 = (bf16[512,256]{1,0:T(8,128)(2,1)S(1)}, bf16[512,256]{1,0:T(8,128)(2,1)}, u32[]{:S(2)}) copy-start(bf16[512,256]{1,0:T(8,128)(2,1)} %param.11) | copy-start | bytes 786436
  528.8 181.8 %all-reduce.2.cloned.1.call-start = ((), (), s32[]{:S(2)}) async-start(), calls=%async_computation.6 | async-start | bytes 524288 | tf_op jit(solution)/shard_map/psum | solution.py:70
Sparse Core Ops, SparseCore 0:
  9.6 31.8 all-gather.2
  228.9 34.4 reduce-scatter.2
  265.8 26.4 all-gather.4
  528.9 50.6 reduce-scatter.4
  585.5 125.0 all-reduce.1
where the time goes:
time: 721 us; the launch traced here: 719 us
  other arithmetic  252 us (35%)
  waiting for transfers between devices  250 us (35%)
  matrix products  110 us (15%)
  local copies, waits for them, and re-layouts  91.8 us (13%)
  between operations  14.5 us (2%)
    scatter-add x8, other arithmetic, accumulate(): return summed.at[places].add(products)  248 us
    psum x1, waiting for transfers between devices, body(): grad_weight = lax.psum(local_weight, ('dom', 'rep'))  127 us
    dot_general x8, matrix products, accumulate(): jnp.einsum(pattern, block_values, picked, preferred_element_type=jnp.floa...  103 us
    gather x8, local copies, waits for them, and re-layouts, accumulate(): picked = jnp.take(source, picks, axis=0)  63.7 us
    reduce_scatter x1, waiting for transfers between devices, body(): lax.psum_scatter(back_partial, 'dom', scatter_dimension=0, tiled=True)  50.8 us
    reduce_scatter x1, waiting for transfers between devices, body(): lax.psum_scatter(partial_value, 'rep', scatter_dimension=0, tiled=True)  34.6 us
    all_gather x1, waiting for transfers between devices, body(): raw_rows = lax.all_gather(node_features, 'dom', axis=0, tiled=True)  32.9 us
    unnamed x14, local copies, waits for them, and re-layouts  25.5 us
  transfers between devices with their start and end apart: 5, of which 5 were waited for; matrix products, arithmetic and copies ran while one was open for 3% of the time, Pallas kernels for 0%

commit v1 on v0

--- a/solution.py
+++ b/solution.py
@@ -67,7 +67,8 @@
         jnp.bfloat16
     )
     local_weight = jnp.dot(node_features.T, grad_projected, preferred_element_type=jnp.float32)
-    grad_weight = lax.psum(local_weight, ("dom", "rep"))
+    half = lax.psum(local_weight, "rep")
+    grad_weight = lax.psum(half, "dom")
     return (output, grad_features, grad_weight)
 
 

time: 721 us -> 693 us (0.961)
  waiting for transfers between devices: 250 us -> 222 us
    psum x1 -> x2, waiting for transfers between devices: 127 us -> 98.4 us  [the longest x1 55.6 us: body(): grad_weight = lax.psum(half, 'dom')]
  transfers between devices with their start and end apart: 5 -> 6, of which waited for: 5 -> 6; matrix products, arithmetic and copies ran while one was open for 3% -> 4% of each run, Pallas kernels for 0% -> 0%
where the time goes in v1:
time: 693 us; the launch traced here: 691 us
  other arithmetic  252 us (36%)
  waiting for transfers between devices  222 us (32%)
  matrix products  110 us (16%)
  local copies, waits for them, and re-layouts  91.8 us (13%)
  between operations  14.8 us (2%)
    scatter-add x8, other arithmetic, accumulate(): return summed.at[places].add(products)  248 us
    dot_general x8, matrix products, accumulate(): jnp.einsum(pattern, block_values, picked, preferred_element_type=jnp.floa...  103 us
    gather x8, local copies, waits for them, and re-layouts, accumulate(): picked = jnp.take(source, picks, axis=0)  63.7 us
    psum x1, waiting for transfers between devices, body(): grad_weight = lax.psum(half, 'dom')  55.6 us
    reduce_scatter x1, waiting for transfers between devices, body(): lax.psum_scatter(back_partial, 'dom', scatter_dimension=0, tiled=True)  50.8 us
    psum x1, waiting for transfers between devices, body(): half = lax.psum(local_weight, 'rep')  42.8 us
    reduce_scatter x1, waiting for transfers between devices, body(): lax.psum_scatter(partial_value, 'rep', scatter_dimension=0, tiled=True)  34.6 us
    all_gather x1, waiting for transfers between devices, body(): raw_rows = lax.all_gather(node_features, 'dom', axis=0, tiled=True)  32.9 us
  transfers between devices with their start and end apart: 6, of which 6 were waited for; matrix products, arithmetic and copies ran while one was open for 4% of the time, Pallas kernels for 0%

profile of v1, /device:TPU:0, one launch (start us, length us, event | category | flops | bytes accessed | tf_op | source)
XLA Modules:
  0.0 690.8 jit_solution(9641742613589210749)
XLA Ops:
  7.2 0.7 all-gather.3.cloned.1.call-update
  8.6 32.9 %all-gather.3.cloned.1.call-done = bf16[4096,256]{1,0:T(8,128)(2,1)} async-done(((bf16[512,256]{1,0:T(8,128)(2,1)}), bf16[4096,256]{1,0:T(8,128)(2,1)}) %all-gather.3.cloned.1.call-update) | async-done | bytes 2097168 | tf_op jit(solution)/shard_map/all_gather | solution.py:44
  41.5 3.7 convolution_convert_fusion
  45.2 0.2 broadcast_in_dim.74
  45.4 181.9 %while.26 = (s32[]{:T(128)}, f32[16,128,256]{2,1,0:T(8,128)S(1)}, s32[512]{0:T(512)S(1)}, bf16[512,128,128]{2,1,0:T(8,128)(2,1)}, s32[512]{0:T(512)S(1)}, /*inde...) while((s32[]{:T(128)}, f32[16,128,256]{2,1,0:T(8,128)S(1)}, ...), condition=%wide.region_2.3_spmd, body=%wide.region_0.2_spmd.sunk | while | flops 1086327040 | bytes 96478248 | solution.py:30
  45.4 0.1 compare_and_fusion.4
  45.5 8.2 %gather_fusion = bf16[128,128,256]{2,1,0:T(8,128)(2,1)} fusion(bf16[32,128,256]{2,1,0:T(8,128)(2,1)} %get-tuple-element.424, s32[1024]{0:T(1024)S(1)} %pad_clamp_fusion.4), kind=kCustom, calls=%fused_computation.clone.1 | custom fusion | bytes 16777728 | tf_op jit(solution)/shard_map/while/body/eval_jaxpr/jit(_take)/gather | solution.py:22
  53.7 12.8 %convolution_multiply_fusion.4 = f32[128,128,256]{2,1,0:T(8,128)} fusion(f32[128]{0:T(128)S(1)} %get-tuple-element.384, bf16[128,128,256]{2,1,0:T(8,128)(2,1)} %gather_fusion, pred[128]{0:T(512)(128)(4,1)S(1)} %get-tuple-element.386, bf16[512,128,128]{2,1,0:T(8,128)(2,1)} %get-tuple-element.422, s32[]{:T(128)S(6)} %select_n.85), kind=kOutput, calls=%fused_computation.4.clone.1 | convolution fusion | flops 1082130432 | bytes 29360772 | tf_op jit(solution)/shard_map/while/body/eval_jaxpr/tab,tbf->taf/dot_general | solution.py:23
  66.6 24.3 %scatter_fusion = f32[16,128,256]{2,1,0:T(8,128)S(1)} fusion(f32[16,128,256]{2,1,0:T(8,128)S(1)} %get-tuple-element.409, s32[128]{0:T(128)S(1)} %compare_select_fusion.8, f32[128,128,256]{2,1,0:T(8,128)} %convolution_multiply_fusion.4), kind=kCustom, calls=%fused_computation.2.clone.1 | custom fusion | flops 4194304 | bytes 50332160 | tf_op jit(solution)/shard_map/while/body/eval_jaxpr/scatter-add | solution.py:27
  90.9 0.1 compare_and_fusion.4
  91.0 8.2 %gather_fusion = bf16[128,128,256]{2,1,0:T(8,128)(2,1)} fusion(bf16[32,128,256]{2,1,0:T(8,128)(2,1)} %get-tuple-element.424, s32[1024]{0:T(1024)S(1)} %pad_clamp_fusion.4), kind=kCustom, calls=%fused_computation.clone.1 | custom fusion | bytes 16777728 | tf_op jit(solution)/shard_map/while/body/eval_jaxpr/jit(_take)/gather | solution.py:22
  99.2 12.8 %convolution_multiply_fusion.4 = f32[128,128,256]{2,1,0:T(8,128)} fusion(f32[128]{0:T(128)S(1)} %get-tuple-element.384, bf16[128,128,256]{2,1,0:T(8,128)(2,1)} %gather_fusion, pred[128]{0:T(512)(128)(4,1)S(1)} %get-tuple-element.386, bf16[512,128,128]{2,1,0:T(8,128)(2,1)} %get-tuple-element.422, s32[]{:T(128)S(6)} %select_n.85), kind=kOutput, calls=%fused_computation.4.clone.1 | convolution fusion | flops 1082130432 | bytes 29360772 | tf_op jit(solution)/shard_map/while/body/eval_jaxpr/tab,tbf->taf/dot_general | solution.py:23
  112.1 24.3 %scatter_fusion = f32[16,128,256]{2,1,0:T(8,128)S(1)} fusion(f32[16,128,256]{2,1,0:T(8,128)S(1)} %get-tuple-element.409, s32[128]{0:T(128)S(1)} %compare_select_fusion.8, f32[128,128,256]{2,1,0:T(8,128)} %convolution_multiply_fusion.4), kind=kCustom, calls=%fused_computation.2.clone.1 | custom fusion | flops 4194304 | bytes 50332160 | tf_op jit(solution)/shard_map/while/body/eval_jaxpr/scatter-add | solution.py:27
  136.4 0.1 compare_and_fusion.4
  136.5 8.2 %gather_fusion = bf16[128,128,256]{2,1,0:T(8,128)(2,1)} fusion(bf16[32,128,256]{2,1,0:T(8,128)(2,1)} %get-tuple-element.424, s32[1024]{0:T(1024)S(1)} %pad_clamp_fusion.4), kind=kCustom, calls=%fused_computation.clone.1 | custom fusion | bytes 16777728 | tf_op jit(solution)/shard_map/while/body/eval_jaxpr/jit(_take)/gather | solution.py:22
  144.7 12.8 %convolution_multiply_fusion.4 = f32[128,128,256]{2,1,0:T(8,128)} fusion(f32[128]{0:T(128)S(1)} %get-tuple-element.384, bf16[128,128,256]{2,1,0:T(8,128)(2,1)} %gather_fusion, pred[128]{0:T(512)(128)(4,1)S(1)} %get-tuple-element.386, bf16[512,128,128]{2,1,0:T(8,128)(2,1)} %get-tuple-element.422, s32[]{:T(128)S(6)} %select_n.85), kind=kOutput, calls=%fused_computation.4.clone.1 | convolution fusion | flops 1082130432 | bytes 29360772 | tf_op jit(solution)/shard_map/while/body/eval_jaxpr/tab,tbf->taf/dot_general | solution.py:23
  157.6 24.3 %scatter_fusion = f32[16,128,256]{2,1,0:T(8,128)S(1)} fusion(f32[16,128,256]{2,1,0:T(8,128)S(1)} %get-tuple-element.409, s32[128]{0:T(128)S(1)} %compare_select_fusion.8, f32[128,128,256]{2,1,0:T(8,128)} %convolution_multiply_fusion.4), kind=kCustom, calls=%fused_computation.2.clone.1 | custom fusion | flops 4194304 | bytes 50332160 | tf_op jit(solution)/shard_map/while/body/eval_jaxpr/scatter-add | solution.py:27
  181.9 0.1 compare_and_fusion.4
  182.0 8.2 %gather_fusion = bf16[128,128,256]{2,1,0:T(8,128)(2,1)} fusion(bf16[32,128,256]{2,1,0:T(8,128)(2,1)} %get-tuple-element.424, s32[1024]{0:T(1024)S(1)} %pad_clamp_fusion.4), kind=kCustom, calls=%fused_computation.clone.1 | custom fusion | bytes 16777728 | tf_op jit(solution)/shard_map/while/body/eval_jaxpr/jit(_take)/gather | solution.py:22
  190.2 12.8 %convolution_multiply_fusion.4 = f32[128,128,256]{2,1,0:T(8,128)} fusion(f32[128]{0:T(128)S(1)} %get-tuple-element.384, bf16[128,128,256]{2,1,0:T(8,128)(2,1)} %gather_fusion, pred[128]{0:T(512)(128)(4,1)S(1)} %get-tuple-element.386, bf16[512,128,128]{2,1,0:T(8,128)(2,1)} %get-tuple-element.422, s32[]{:T(128)S(6)} %select_n.85), kind=kOutput, calls=%fused_computation.4.clone.1 | convolution fusion | flops 1082130432 | bytes 29360772 | tf_op jit(solution)/shard_map/while/body/eval_jaxpr/tab,tbf->taf/dot_general | solution.py:23
  203.1 24.3 %scatter_fusion = f32[16,128,256]{2,1,0:T(8,128)S(1)} fusion(f32[16,128,256]{2,1,0:T(8,128)S(1)} %get-tuple-element.409, s32[128]{0:T(128)S(1)} %compare_select_fusion.8, f32[128,128,256]{2,1,0:T(8,128)} %convolution_multiply_fusion.4), kind=kCustom, calls=%fused_computation.2.clone.1 | custom fusion | flops 4194304 | bytes 50332160 | tf_op jit(solution)/shard_map/while/body/eval_jaxpr/scatter-add | solution.py:27
  227.4 1.3 copy-done.1
  228.8 34.6 %reduce-scatter.3.cloned.1.call-done = f32[512,256]{1,0:T(8,128)} async-done(((f32[2048,256]{1,0:T(8,128)}), f32[512,256]{1,0:T(8,128)}) %reduce-scatter.3.cloned.1.call-update) | async-done | bytes 524304 | tf_op jit(solution)/shard_map/reduce_scatter | solution.py:49
  263.4 2.1 multiply_convert_fusion
  265.5 0.2 reduce-scatter.5.cloned.1.call-start
  265.7 22.4 %copy.10 = bf16[1,1,512,128,128]{3,4,2,1,0:T(8,128)(2,1)} copy(bf16[1,1,512,128,128]{4,3,2,1,0:T(8,128)(2,1)} %bitcast.21) | data formatting | bytes 33554432 | tf_op args[5]
  288.1 4.3 all-gather.5.cloned.1.call-done
  292.4 2.4 broadcast_in_dim.75
  294.8 234.0 %while.27 = (s32[]{:T(128)}, f32[32,128,256]{2,1,0:T(8,128)}, s32[512]{0:T(512)S(1)}, bf16[512,128,128]{1,2,0:T(8,128)(2,1)}, s32[512]{0:T(512)S(1)}, /*index=5*...) while((s32[]{:T(128)}, f32[32,128,256]{2,1,0:T(8,128)}, ...), condition=%wide.region_6.7_spmd, body=%wide.region_4.6_spmd.sunk | while | flops 1086327040 | bytes 96478248 | solution.py:30
  294.9 7.8 %gather_fusion.1 = bf16[128,128,256]{2,1,0:T(8,128)(2,1)} fusion(bf16[16,128,256]{2,1,0:T(8,128)(2,1)} %get-tuple-element.457, s32[1024]{0:T(1024)S(1)} %pad_clamp_fusion.5), kind=kCustom, calls=%fused_computation.1.clone.1 | custom fusion | bytes 16777728 | tf_op jit(solution)/shard_map/while/body/eval_jaxpr/jit(_take)/gather | solution.py:22
  302.7 12.8 %convolution_multiply_fusion.5 = f32[128,128,256]{2,1,0:T(8,128)} fusion(f32[128]{0:T(128)S(1)} %get-tuple-element.394, bf16[128,128,256]{2,1,0:T(8,128)(2,1)} %gather_fusion.1, pred[128]{0:T(512)(128)(4,1)S(1)} %get-tuple-element.396, bf16[512,128,128]{1,2,0:T(8,128)(2,1)} %get-tuple-element.455, s32[]{:T(128)S(6)} %select_n.88), kind=kOutput, calls=%fused_computation.16.clone.1 | convolution fusion | flops 1082130432 | bytes 29360772 | tf_op jit(solution)/shard_map/while/body/eval_jaxpr/tba,tbf->taf/dot_general | solution.py:23
  315.5 37.9 %scatter_fusion.1 = f32[32,128,256]{2,1,0:T(8,128)} fusion(f32[32,128,256]{2,1,0:T(8,128)} %get-tuple-element.442, s32[128]{0:T(128)S(1)} %compare_select_fusion.9, f32[128,128,256]{2,1,0:T(8,128)} %convolution_multiply_fusion.5), kind=kCustom, calls=%fused_computation.3.clone.1 | custom fusion | flops 4194304 | bytes 50332160 | tf_op jit(solution)/shard_map/while/body/eval_jaxpr/scatter-add | solution.py:27
  353.5 7.8 %gather_fusion.1 = bf16[128,128,256]{2,1,0:T(8,128)(2,1)} fusion(bf16[16,128,256]{2,1,0:T(8,128)(2,1)} %get-tuple-element.457, s32[1024]{0:T(1024)S(1)} %pad_clamp_fusion.5), kind=kCustom, calls=%fused_computation.1.clone.1 | custom fusion | bytes 16777728 | tf_op jit(solution)/shard_map/while/body/eval_jaxpr/jit(_take)/gather | solution.py:22
  361.2 12.8 %convolution_multiply_fusion.5 = f32[128,128,256]{2,1,0:T(8,128)} fusion(f32[128]{0:T(128)S(1)} %get-tuple-element.394, bf16[128,128,256]{2,1,0:T(8,128)(2,1)} %gather_fusion.1, pred[128]{0:T(512)(128)(4,1)S(1)} %get-tuple-element.396, bf16[512,128,128]{1,2,0:T(8,128)(2,1)} %get-tuple-element.455, s32[]{:T(128)S(6)} %select_n.88), kind=kOutput, calls=%fused_computation.16.clone.1 | convolution fusion | flops 1082130432 | bytes 29360772 | tf_op jit(solution)/shard_map/while/body/eval_jaxpr/tba,tbf->taf/dot_general | solution.py:23
  374.1 37.7 %scatter_fusion.1 = f32[32,128,256]{2,1,0:T(8,128)} fusion(f32[32,128,256]{2,1,0:T(8,128)} %get-tuple-element.442, s32[128]{0:T(128)S(1)} %compare_select_fusion.9, f32[128,128,256]{2,1,0:T(8,128)} %convolution_multiply_fusion.5), kind=kCustom, calls=%fused_computation.3.clone.1 | custom fusion | flops 4194304 | bytes 50332160 | tf_op jit(solution)/shard_map/while/body/eval_jaxpr/scatter-add | solution.py:27
  411.9 7.8 %gather_fusion.1 = bf16[128,128,256]{2,1,0:T(8,128)(2,1)} fusion(bf16[16,128,256]{2,1,0:T(8,128)(2,1)} %get-tuple-element.457, s32[1024]{0:T(1024)S(1)} %pad_clamp_fusion.5), kind=kCustom, calls=%fused_computation.1.clone.1 | custom fusion | bytes 16777728 | tf_op jit(solution)/shard_map/while/body/eval_jaxpr/jit(_take)/gather | solution.py:22
  419.7 12.8 %convolution_multiply_fusion.5 = f32[128,128,256]{2,1,0:T(8,128)} fusion(f32[128]{0:T(128)S(1)} %get-tuple-element.394, bf16[128,128,256]{2,1,0:T(8,128)(2,1)} %gather_fusion.1, pred[128]{0:T(512)(128)(4,1)S(1)} %get-tuple-element.396, bf16[512,128,128]{1,2,0:T(8,128)(2,1)} %get-tuple-element.455, s32[]{:T(128)S(6)} %select_n.88), kind=kOutput, calls=%fused_computation.16.clone.1 | convolution fusion | flops 1082130432 | bytes 29360772 | tf_op jit(solution)/shard_map/while/body/eval_jaxpr/tba,tbf->taf/dot_general | solution.py:23
  432.6 37.6 %scatter_fusion.1 = f32[32,128,256]{2,1,0:T(8,128)} fusion(f32[32,128,256]{2,1,0:T(8,128)} %get-tuple-element.442, s32[128]{0:T(128)S(1)} %compare_select_fusion.9, f32[128,128,256]{2,1,0:T(8,128)} %convolution_multiply_fusion.5), kind=kCustom, calls=%fused_computation.3.clone.1 | custom fusion | flops 4194304 | bytes 50332160 | tf_op jit(solution)/shard_map/while/body/eval_jaxpr/scatter-add | solution.py:27
  470.2 0.1 compare_and_fusion.5
  470.3 7.8 %gather_fusion.1 = bf16[128,128,256]{2,1,0:T(8,128)(2,1)} fusion(bf16[16,128,256]{2,1,0:T(8,128)(2,1)} %get-tuple-element.457, s32[1024]{0:T(1024)S(1)} %pad_clamp_fusion.5), kind=kCustom, calls=%fused_computation.1.clone.1 | custom fusion | bytes 16777728 | tf_op jit(solution)/shard_map/while/body/eval_jaxpr/jit(_take)/gather | solution.py:22
  478.0 12.8 %convolution_multiply_fusion.5 = f32[128,128,256]{2,1,0:T(8,128)} fusion(f32[128]{0:T(128)S(1)} %get-tuple-element.394, bf16[128,128,256]{2,1,0:T(8,128)(2,1)} %gather_fusion.1, pred[128]{0:T(512)(128)(4,1)S(1)} %get-tuple-element.396, bf16[512,128,128]{1,2,0:T(8,128)(2,1)} %get-tuple-element.455, s32[]{:T(128)S(6)} %select_n.88), kind=kOutput, calls=%fused_computation.16.clone.1 | convolution fusion | flops 1082130432 | bytes 29360772 | tf_op jit(solution)/shard_map/while/body/eval_jaxpr/tba,tbf->taf/dot_general | solution.py:23
  490.9 37.9 %scatter_fusion.1 = f32[32,128,256]{2,1,0:T(8,128)} fusion(f32[32,128,256]{2,1,0:T(8,128)} %get-tuple-element.442, s32[128]{0:T(128)S(1)} %compare_select_fusion.9, f32[128,128,256]{2,1,0:T(8,128)} %convolution_multiply_fusion.5), kind=kCustom, calls=%fused_computation.3.clone.1 | custom fusion | flops 4194304 | bytes 50332160 | tf_op jit(solution)/shard_map/while/body/eval_jaxpr/scatter-add | solution.py:27
  528.8 50.8 %reduce-scatter.5.cloned.1.call-done = f32[512,256]{1,0:T(8,128)} async-done(((f32[4096,256]{1,0:T(8,128)}), f32[512,256]{1,0:T(8,128)}) %reduce-scatter.5.cloned.1.call-update) | async-done | bytes 524304 | tf_op jit(solution)/shard_map/reduce_scatter | solution.py:63
  579.6 2.0 convolution_bitcast_fusion
  581.7 42.8 %all-reduce.3.cloned.1.call-done = f32[256,256]{0,1:T(8,128)} async-done(((f32[256,256]{0,1:T(8,128)}), f32[256,256]{0,1:T(8,128)}) %all-reduce.3.cloned.1.call-update) | async-done | bytes 262160 | tf_op jit(solution)/shard_map/psum | solution.py:70
  624.5 2.0 convolution_convert_fusion.1
  626.6 55.6 %all-reduce.5.cloned.1.call-done = f32[256,256]{0,1:T(8,128)} async-done(((f32[256,256]{0,1:T(8,128)}), f32[256,256]{0,1:T(8,128)}) %all-reduce.5.cloned.1.call-update) | async-done | bytes 262160 | tf_op jit(solution)/shard_map/psum | solution.py:71
  682.1 1.8 copy.12
  (41 shorter events, 1.2 us)
Async XLA Ops:
  7.2 34.4 %copy-start = (bf16[256,256]{1,0:T(8,128)(2,1)S(1)}, bf16[256,256]{1,0:T(8,128)(2,1)}, u32[]{:S(2)}) copy-start(bf16[256,256]{1,0:T(8,128)(2,1)} %param.12) | copy-start | bytes 393220
  7.2 38.2 %copy-start.4 = (s32[1,1,512]{2,1,0:T(1,128)S(1)}, s32[1,1,512]{2,1,0:T(1,128)}, u32[]{:S(2)}) copy-start(s32[1,1,512]{2,1,0:T(1,128)} %param.14) | copy-start | bytes 6148
  7.2 38.2 %copy-start.5 = (s32[1,1,512]{2,1,0:T(1,128)S(1)}, s32[1,1,512]{2,1,0:T(1,128)}, u32[]{:S(2)}) copy-start(s32[1,1,512]{2,1,0:T(1,128)} %param.15) | copy-start | bytes 6148
  7.2 34.3 %all-gather.3.cloned.1.call-start = ((), (), s32[]{:S(2)}) async-start(), calls=%async_computation.2 | async-start | bytes 2359296 | tf_op jit(solution)/shard_map/all_gather | solution.py:44
  7.9 255.5 %reduce-scatter.3.cloned.1.call-start = ((), (), s32[]{:S(2)}) async-start(), calls=%async_computation.3 | async-start | bytes 2621440 | tf_op jit(solution)/shard_map/reduce_scatter | solution.py:49
  45.4 218.0 %copy-start.3 = (bf16[512,256]{1,0:T(8,128)(2,1)S(1)}, bf16[512,256]{1,0:T(8,128)(2,1)}, u32[]{:S(2)}) copy-start(bf16[512,256]{1,0:T(8,128)(2,1)} %param.13) | copy-start | bytes 786436
  227.4 1.3 copy-start.1
  228.7 63.6 %all-gather.5.cloned.1.call-start = ((), (), s32[]{:S(2)}) async-start(), calls=%async_computation.4 | async-start | bytes 1310720 | tf_op jit(solution)/shard_map/all_gather | solution.py:52
  265.5 314.1 %reduce-scatter.5.cloned.1.call-start = ((), (), s32[]{:S(2)}) async-start(), calls=%async_computation.5 | async-start | bytes 4718592 | tf_op jit(solution)/shard_map/reduce_scatter | solution.py:63
  294.8 284.8 %copy-start.2 = (bf16[512,256]{1,0:T(8,128)(2,1)S(1)}, bf16[512,256]{1,0:T(8,128)(2,1)}, u32[]{:S(2)}) copy-start(bf16[512,256]{1,0:T(8,128)(2,1)} %param.11) | copy-start | bytes 786436
  528.8 95.7 %all-reduce.3.cloned.1.call-start = ((), (), s32[]{:S(2)}) async-start(), calls=%async_computation.6 | async-start | bytes 524288 | tf_op jit(solution)/shard_map/psum | solution.py:70
  581.6 100.5 %all-reduce.5.cloned.1.call-start = ((), (), s32[]{:S(2)}) async-start(), calls=%async_computation.7 | async-start | bytes 524288 | tf_op jit(solution)/shard_map/psum | solution.py:71
Sparse Core Ops, SparseCore 0:
  9.6 31.8 all-gather.2
  228.9 34.4 reduce-scatter.2
  265.8 26.4 all-gather.4
  528.9 50.6 reduce-scatter.4
  583.0 41.5 all-reduce.2
  626.7 55.4 all-reduce.4
